TPU v7x, 32 devices: a whole 2x2x4 slice. The times are simulated.
32 devices in a mesh: groups: 2 (over x), row: 8 (over z, y), col: 2 (over core).
Axes of the slice: x: 2, y: 2, z: 4, core: 2. Of those that a mesh axis runs over, the one named last changes fastest.
Arguments:
- queries: bfloat16 [8192, 1024], P(('groups', 'row', 'col')), parts along dimension 0, may hold values from -200 to 200
- keys: bfloat16 [8192, 128], P(('groups', 'row', 'col')), parts along dimension 0, may hold values from -5 to 5
- values: bfloat16 [8192, 128], P(('groups', 'row', 'col')), parts along dimension 0, may hold values from -6 to 6
- doc_lengths: int32 [32], P('groups'), parts along dimension 0, may hold values from 1 to 3072, 4096 in all
Outputs:
- attended: bfloat16 [8192, 1024], P(('groups', 'row', 'col')), parts along dimension 0
There are 2 independent parts, one for each index of `groups`. A program takes and returns all parts, laid end to end along the dimension named above; each array names one. Nothing has to cross between parts.
Inputs may be any that keep to these rules, and one draw needn't show every extreme that they name: `doc_lengths`: the 16 lengths sum to 4096 and the longest is exactly 3072.
All inputs are finite; a program needn't handle non-finite values.
Results may differ from a plain program's by a relative error of at most 0.0055.
Values may be sent and summed in bfloat16 or wider, within the bound.
A program may use at most 64 MiB of HBM per device.

v0:
```python
import functools

import jax
import jax.numpy as jnp
from jax import lax
from jax.experimental import pallas as pl
from jax.experimental.pallas import tpu as pltpu
from jax.sharding import PartitionSpec as P

HEAD_DIM = 128
RATE = HEAD_DIM ** (-0.5) * 1.4426950408889634
MASKED = -1e30


def kernel(
    n_row,
    n_col,
    lanes,
    reach,
    lens_ref,
    q_ref,
    k_ref,
    v_ref,
    o_ref,
    kbuf,
    vbuf,
    top_ref,
    total_ref,
    acc_ref,
    in_sem,
    mate_sem,
    up_send,
    cross_send,
    mate_send,
):
    shard = q_ref.shape[0]
    heads = q_ref.shape[1] // HEAD_DIM
    levels = n_row // lanes
    steps = 2 * (min(levels - 1, (reach + lanes - 1) // lanes) + 1)
    row = lax.axis_index("row")
    col = lax.axis_index("col")
    level = row // lanes
    lane = row % lanes
    mate = 1 - col
    other = level * lanes + (lanes - 1 - lane)
    mine = pl.ds(pl.multiple_of(col * shard, shard), shard)
    theirs = pl.ds(pl.multiple_of(mate * shard, shard), shard)

    def needs(reader, source):
        return (source >= 0) & (reader > source) & (reader - source <= reach)

    has_up = level + 1 < levels
    has_down = level > 0
    has_other = lanes > 1

    barrier = pltpu.get_barrier_semaphore()
    pl.semaphore_signal(barrier, inc=1, device_id={"col": mate})
    if has_other:
        pl.semaphore_signal(barrier, inc=1, device_id={"row": other})

    @pl.when(has_up)
    def _():
        pl.semaphore_signal(barrier, inc=1, device_id={"row": row + lanes})

    @pl.when(has_down)
    def _():
        pl.semaphore_signal(barrier, inc=1, device_id={"row": row - lanes})

    count = 1 + int(has_other) + has_up.astype(jnp.int32) + has_down.astype(jnp.int32)
    pl.semaphore_wait(barrier, count)

    def send(src, buf, source, which, j, sends, recvs, at, device):
        return pltpu.make_async_remote_copy(
            src_ref=src,
            dst_ref=buf.at[source, mine, :],
            send_sem=sends.at[which, j],
            recv_sem=recvs.at[which, at],
            device_id=device,
            device_id_type=pl.DeviceIdType.MESH,
        )

    def source_of(j):
        dist, kind = j // 2, j % 2
        cross = kind == 1
        from_lane = jnp.where(cross, lanes - 1 - lane, lane)
        source = (level - dist) * lanes + from_lane
        if lanes == 1:
            source = jnp.where(cross, -1, source)
        return source

    def relays(j, source, straight):
        mate_wants = (source < row) | (col < mate)
        found = [(mate_wants, mate_send, mate_sem, j, {"col": mate})]
        up = straight & has_up & needs(row + lanes, source)
        found.append((up, up_send, in_sem, j + 2, {"row": row + lanes}))
        if has_other:
            cross = straight & needs(other, source)
            found.append((cross, cross_send, in_sem, j + 1, {"row": other}))
        return found

    def forward(src, buf, source, which, j, straight):
        for wanted, sends, recvs, at, device in reversed(relays(j, source, straight)):

            @pl.when(wanted)
            def _():
                send(src, buf, source, which, j, sends, recvs, at, device).start()

    def arrived(buf, source, which, j, sems, part):
        here = buf.at[source, part, :]
        pltpu.make_async_copy(here, here, sems.at[which, j]).wait()

    forward(k_ref, kbuf, row, 0, 0, True)
    forward(v_ref, vbuf, row, 1, 0, True)

    first = (row * n_col + col) * shard
    qpos = first + lax.broadcasted_iota(jnp.int32, (1, shard), 1)
    begin = jnp.zeros((1, shard), jnp.int32)
    end = jnp.int32(0)
    for doc in range(lens_ref.shape[0]):
        length = lens_ref[doc]
        end = end + length
        begin = begin + jnp.where(qpos >= end, length, 0)

    def attend(kblock, vblock, kfirst, fresh):
        count = kblock.shape[0]
        kpos = kfirst + lax.broadcasted_iota(jnp.int32, (count, shard), 0)
        seen = kpos >= begin
        if fresh:
            seen = seen & (kpos <= qpos)
        bias = jnp.where(seen, jnp.float32(0.0), jnp.float32(MASKED))
        vflip = vblock.T
        for head in range(heads):
            qhead = q_ref[:, head * HEAD_DIM : (head + 1) * HEAD_DIM]
            scores = lax.dot_general(
                kblock, qhead, (((1,), (1,)), ((), ())), preferred_element_type=jnp.float32
            )
            scores = scores + bias
            top = jnp.max(scores, axis=0, keepdims=True)
            if not fresh:
                before = top_ref[head : head + 1, :]
                top = jnp.maximum(before, top)
            weights = jnp.exp2((scores - top) * RATE)
            total = jnp.sum(weights, axis=0, keepdims=True)
            summed = jnp.dot(
                vflip, weights.astype(jnp.bfloat16), preferred_element_type=jnp.float32
            )
            if not fresh:
                factor = jnp.exp2((before - top) * RATE)
                total = total + total_ref[head : head + 1, :] * factor
                summed = summed + acc_ref[head] * factor
            top_ref[head : head + 1, :] = top
            total_ref[head : head + 1, :] = total
            acc_ref[head] = summed

    attend(k_ref[...], v_ref[...], first, True)

    @pl.when(col > 0)
    def _():
        arrived(kbuf, row, 0, 0, mate_sem, theirs)
        arrived(vbuf, row, 1, 0, mate_sem, theirs)
        attend(kbuf[row, :shard, :], vbuf[row, :shard, :], row * n_col * shard, False)

    @pl.loop(1, steps)
    def _(j):
        source = source_of(j)

        @pl.when(needs(row, source))
        def _():
            straight = j % 2 == 0
            for which, buf in enumerate((kbuf, vbuf)):
                arrived(buf, source, which, j, in_sem, mine)
                forward(buf.at[source, mine, :], buf, source, which, j, straight)
            arrived(kbuf, source, 0, j, mate_sem, theirs)
            arrived(vbuf, source, 1, j, mate_sem, theirs)
            attend(kbuf[source], vbuf[source], source * n_col * shard, False)

    for head in range(heads):
        inverse = 1.0 / total_ref[head : head + 1, :]
        result = (acc_ref[head] * inverse).T
        o_ref[:, head * HEAD_DIM : (head + 1) * HEAD_DIM] = result.astype(o_ref.dtype)

    @pl.loop(0, steps)
    def _(j):
        source = source_of(j)

        @pl.when(needs(row, source) | (j == 0))
        def _():
            for wanted, sends, recvs, at, device in relays(j, source, j % 2 == 0):

                @pl.when(wanted)
                def _():
                    for which, buf in enumerate((kbuf, vbuf)):
                        part = buf.at[source, mine, :]
                        send(part, buf, source, which, j, sends, recvs, at, device).wait_send()


def shards(n_row, n_col, queries, keys, values, doc_lengths):
    shard, width = queries.shape
    lanes = 2 if n_row % 2 == 0 else 1
    span = shard * n_row * n_col
    longest = (3 * span) // 4
    reach = min(n_row - 1, -(-longest // (shard * n_col)))
    levels = n_row // lanes
    steps = 2 * (min(levels - 1, (reach + lanes - 1) // lanes) + 1)
    tile = shard * n_col
    heads = width // HEAD_DIM
    vmem = pl.BlockSpec(memory_space=pltpu.VMEM)
    sems = pltpu.SemaphoreType.DMA((2, steps))
    return pl.pallas_call(
        functools.partial(kernel, n_row, n_col, lanes, reach),
        out_shape=jax.ShapeDtypeStruct(queries.shape, queries.dtype),
        in_specs=[pl.BlockSpec(memory_space=pltpu.SMEM), vmem, vmem, vmem],
        out_specs=vmem,
        scratch_shapes=[
            pltpu.VMEM((n_row, tile, HEAD_DIM), keys.dtype),
            pltpu.VMEM((n_row, tile, HEAD_DIM), values.dtype),
            pltpu.VMEM((heads, shard), jnp.float32),
            pltpu.VMEM((heads, shard), jnp.float32),
            pltpu.VMEM((heads, HEAD_DIM, shard), jnp.float32),
            sems,
            sems,
            sems,
            sems,
            sems,
        ],
        compiler_params=pltpu.CompilerParams(
            collective_id=0, has_side_effects=True, vmem_limit_bytes=60 << 20
        ),
        name="attend",
    )(doc_lengths, queries, keys, values)


def solution(mesh):
    placed = P(("groups", "row", "col"), None)
    return jax.shard_map(
        functools.partial(shards, mesh.shape["row"], mesh.shape["col"]),
        mesh=mesh,
        in_specs=(placed, placed, placed, P("groups")),
        out_specs=placed,
        check_vma=False,
    )
```

profile of v0, /device:TPU:25, one launch (start us, length us, event | category | flops | bytes accessed | tf_op | source)
XLA Modules:
  0.0 43.0 jit_solution(2767081714217333002)
XLA Ops:
  0.0 41.1 %attend.1 = bf16[256,1024]{1,0:T(8,128)(2,1)} custom-call(s32[16]{0:T(128)} %lens_ref.1, bf16[256,1024]{1,0:T(8,128)(2,1)} %q_ref.1, bf16[256,128]{1,0:T(8,128)(2,1)} %k_ref.1, bf16[256,128]{1,0:T(8,128)(2,1)} %v_ref.1), custom_call_target="tpu_custom_call" | custom-call | tf_op jit(solution)/shard_map/attend/pallas_call | solution.py:209
  41.1 1.9 %copy.6 = bf16[256,1024]{1,0:T(8,128)(2,1)} copy(bf16[256,1024]{1,0:T(8,128)(2,1)} %attend.1) | data formatting | bytes 1048576
where the time goes:
time: 43.2 us; the launch traced here: 43 us
  Pallas kernels  41.1 us (95%)
  local copies, waits for them, and re-layouts  1.87 us (4%)
    pallas_call x1, Pallas kernels, shards(): pl.pallas_call(functools.partial(kernel, n_row, n_col, lanes, reach), out...  41.1 us
    unnamed x1, local copies, waits for them, and re-layouts  1.87 us

commit v1 on v0

--- a/solution.py
+++ b/solution.py
@@ -27,6 +27,9 @@
     top_ref,
     total_ref,
     acc_ref,
+    qa_ref,
+    s_ref,
+    load_sem,
     in_sem,
     mate_sem,
     up_send,
@@ -66,6 +69,18 @@
     def _():
         pl.semaphore_signal(barrier, inc=1, device_id={"row": row - lanes})
 
+    loads = [
+        pltpu.make_async_copy(k_ref, kbuf.at[row, mine, :], load_sem.at[0]),
+        pltpu.make_async_copy(v_ref, vbuf.at[row, mine, :], load_sem.at[1]),
+    ]
+    for head in range(heads):
+        part = q_ref.at[:, head * HEAD_DIM : (head + 1) * HEAD_DIM]
+        loads.append(
+            pltpu.make_async_copy(part, qa_ref.at[head, :, :HEAD_DIM], load_sem.at[2 + head])
+        )
+    for load in loads:
+        load.start()
+
     count = 1 + int(has_other) + has_up.astype(jnp.int32) + has_down.astype(jnp.int32)
     pl.semaphore_wait(barrier, count)
 
@@ -114,32 +129,55 @@
 
     first = (row * n_col + col) * shard
     qpos = first + lax.broadcasted_iota(jnp.int32, (1, shard), 1)
-    begin = jnp.zeros((1, shard), jnp.int32)
+
+    def within(places):
+        return (places >= begins) & (places < ends)
+
+    lanes_of = lax.broadcasted_iota(jnp.int32, (1, HEAD_DIM), 1)
+    begins = jnp.zeros((1, HEAD_DIM), jnp.int32)
+    ends = jnp.full((1, HEAD_DIM), n_row * n_col * shard, jnp.int32)
     end = jnp.int32(0)
-    for doc in range(lens_ref.shape[0]):
-        length = lens_ref[doc]
-        end = end + length
-        begin = begin + jnp.where(qpos >= end, length, 0)
+    docs = lens_ref.shape[0]
+    for doc in range(docs):
+        begins = jnp.where(lanes_of == doc, end, begins)
+        end = end + lens_ref[doc]
+        ends = jnp.where(lanes_of == doc, end, ends)
+    qplace = first + lax.broadcasted_iota(jnp.int32, (shard, HEAD_DIM), 0)
+    member = jnp.where(within(qplace) & (lanes_of < docs), 1.0, 0.0).astype(jnp.bfloat16)
+    for head in range(heads):
+        qa_ref[head, :, HEAD_DIM:] = member
+    for load in loads:
+        load.wait()
 
     def attend(kblock, vblock, kfirst, fresh):
         count = kblock.shape[0]
-        kpos = kfirst + lax.broadcasted_iota(jnp.int32, (count, shard), 0)
-        seen = kpos >= begin
+        kplace = kfirst + lax.broadcasted_iota(jnp.int32, (count, HEAD_DIM), 0)
+        apart = jnp.where(within(kplace), 0.0, MASKED).astype(jnp.bfloat16)
+        kwide = jnp.concatenate([kblock, apart], axis=1)
         if fresh:
-            seen = seen & (kpos <= qpos)
-        bias = jnp.where(seen, jnp.float32(0.0), jnp.float32(MASKED))
+            kpos = kfirst + lax.broadcasted_iota(jnp.int32, (count, shard), 0)
+            bias = jnp.where(kpos <= qpos, jnp.float32(0.0), jnp.float32(MASKED))
         vflip = vblock.T
+
+        def score(head):
+            scores = lax.dot_general(
+                kwide, qa_ref[head], (((1,), (1,)), ((), ())), preferred_element_type=jnp.float32
+            )
+            if fresh:
+                scores = scores + bias
+            s_ref[head % 2, :count, :] = scores
+            top = jnp.max(scores, axis=0, keepdims=True)
+            if fresh:
+                return top, top
+            before = top_ref[head : head + 1, :]
+            return before, jnp.maximum(before, top)
+
+        ahead = score(0)
         for head in range(heads):
-            qhead = q_ref[:, head * HEAD_DIM : (head + 1) * HEAD_DIM]
-            scores = lax.dot_general(
-                kblock, qhead, (((1,), (1,)), ((), ())), preferred_element_type=jnp.float32
-            )
-            scores = scores + bias
-            top = jnp.max(scores, axis=0, keepdims=True)
-            if not fresh:
-                before = top_ref[head : head + 1, :]
-                top = jnp.maximum(before, top)
-            weights = jnp.exp2((scores - top) * RATE)
+            before, top = ahead
+            if head + 1 < heads:
+                ahead = score(head + 1)
+            weights = jnp.exp2((s_ref[head % 2, :count, :] - top) * RATE)
             total = jnp.sum(weights, axis=0, keepdims=True)
             summed = jnp.dot(
                 vflip, weights.astype(jnp.bfloat16), preferred_element_type=jnp.float32
@@ -152,7 +190,7 @@
             total_ref[head : head + 1, :] = total
             acc_ref[head] = summed
 
-    attend(k_ref[...], v_ref[...], first, True)
+    attend(kbuf[row, mine, :], vbuf[row, mine, :], first, True)
 
     @pl.when(col > 0)
     def _():
@@ -205,11 +243,12 @@
     tile = shard * n_col
     heads = width // HEAD_DIM
     vmem = pl.BlockSpec(memory_space=pltpu.VMEM)
+    whole = pl.BlockSpec(memory_space=pltpu.HBM)
     sems = pltpu.SemaphoreType.DMA((2, steps))
     return pl.pallas_call(
         functools.partial(kernel, n_row, n_col, lanes, reach),
         out_shape=jax.ShapeDtypeStruct(queries.shape, queries.dtype),
-        in_specs=[pl.BlockSpec(memory_space=pltpu.SMEM), vmem, vmem, vmem],
+        in_specs=[pl.BlockSpec(memory_space=pltpu.SMEM), whole, whole, whole],
         out_specs=vmem,
         scratch_shapes=[
             pltpu.VMEM((n_row, tile, HEAD_DIM), keys.dtype),
@@ -217,6 +256,9 @@
             pltpu.VMEM((heads, shard), jnp.float32),
             pltpu.VMEM((heads, shard), jnp.float32),
             pltpu.VMEM((heads, HEAD_DIM, shard), jnp.float32),
+            pltpu.VMEM((heads, shard, 2 * HEAD_DIM), queries.dtype),
+            pltpu.VMEM((2, tile, shard), jnp.float32),
+            pltpu.SemaphoreType.DMA((2 + heads,)),
             sems,
             sems,
             sems,
@@ -224,7 +266,7 @@
             sems,
         ],
         compiler_params=pltpu.CompilerParams(
-            collective_id=0, has_side_effects=True, vmem_limit_bytes=60 << 20
+            collective_id=0, has_side_effects=True, vmem_limit_bytes=24 << 20
         ),
         name="attend",
     )(doc_lengths, queries, keys, values)

time: 43.2 us -> 36.8 us (0.85)
  Pallas kernels: 41.1 us -> 32.4 us
  local copies, waits for them, and re-layouts: 1.87 us -> 4.17 us
    pallas_call x1, Pallas kernels: 41.1 us -> 32.4 us  [shards(): pl.pallas_call(functools.partial(kernel, n_row, n_col, lanes, reach), out...]
    unnamed x1 -> x9, local copies, waits for them, and re-layouts: 1.87 us -> 4.17 us
where the time goes in v1:
time: 36.8 us; the launch traced here: 36.6 us
  Pallas kernels  32.4 us (88%)
  local copies, waits for them, and re-layouts  4.17 us (11%)
    pallas_call x1, Pallas kernels, shards(): pl.pallas_call(functools.partial(kernel, n_row, n_col, lanes, reach), out...  32.4 us
    unnamed x9, local copies, waits for them, and re-layouts  4.17 us

profile of v1, /device:TPU:25, one launch (start us, length us, event | category | flops | bytes accessed | tf_op | source)
XLA Modules:
  0.0 36.6 jit_solution(557521976351226634)
XLA Ops:
  0.0 0.0 copy-start
  0.0 1.0 %copy-done = bf16[256,1024]{1,0:T(8,128)(2,1)S(1)} copy-done((bf16[256,1024]{1,0:T(8,128)(2,1)S(1)}, bf16[256,1024]{1,0:T(8,128)(2,1)}, u32[]{:S(2)}) %copy-start) | copy-done | bytes 524312
  1.0 0.0 copy-start.1
  1.0 0.8 %copy-done.1 = bf16[256,128]{1,0:T(8,128)(2,1)S(1)} copy-done((bf16[256,128]{1,0:T(8,128)(2,1)S(1)}, bf16[256,128]{1,0:T(8,128)(2,1)}, u32[]{:S(2)}) %copy-start.1) | copy-done | bytes 65560
  1.9 0.0 copy-start.2
  1.9 0.8 %copy-done.2 = bf16[256,128]{1,0:T(8,128)(2,1)S(1)} copy-done((bf16[256,128]{1,0:T(8,128)(2,1)S(1)}, bf16[256,128]{1,0:T(8,128)(2,1)}, u32[]{:S(2)}) %copy-start.2) | copy-done | bytes 65560
  2.7 0.0 copy-start.3
  2.7 0.7 %copy-done.3 = s32[16]{0:T(128)S(1)} copy-done((s32[16]{0:T(128)S(1)}, s32[16]{0:T(128)}, u32[]{:S(2)}) %copy-start.3) | copy-done | bytes 88
  3.4 32.4 %attend.1 = bf16[256,1024]{1,0:T(8,128)(2,1)S(1)} custom-call(s32[16]{0:T(128)S(1)} %copy-done.3, bf16[256,1024]{1,0:T(8,128)(2,1)S(1)} %copy-done, bf16[256,128]{1,0:T(8,128)(2,1)S(1)} %copy-done.1, bf16[256,128]{1,0:T(8,128)(2,1)S(1)} %copy-done.2), custom_call_target="tpu_custom_call" | custom-call | tf_op jit(solution)/shard_map/attend/pallas_call | solution.py:248
  35.8 0.8 %copy.6 = bf16[256,1024]{1,0:T(8,128)(2,1)} copy(bf16[256,1024]{1,0:T(8,128)(2,1)S(1)} %attend.1) | data formatting | bytes 1048576
Async XLA Ops:
  0.0 1.0 %copy-start = (bf16[256,1024]{1,0:T(8,128)(2,1)S(1)}, bf16[256,1024]{1,0:T(8,128)(2,1)}, u32[]{:S(2)}) copy-start(bf16[256,1024]{1,0:T(8,128)(2,1)} %q_ref.1) | copy-start | bytes 1572868
  1.0 0.8 %copy-start.1 = (bf16[256,128]{1,0:T(8,128)(2,1)S(1)}, bf16[256,128]{1,0:T(8,128)(2,1)}, u32[]{:S(2)}) copy-start(bf16[256,128]{1,0:T(8,128)(2,1)} %k_ref.1) | copy-start | bytes 196612
  1.9 0.8 %copy-start.2 = (bf16[256,128]{1,0:T(8,128)(2,1)S(1)}, bf16[256,128]{1,0:T(8,128)(2,1)}, u32[]{:S(2)}) copy-start(bf16[256,128]{1,0:T(8,128)(2,1)} %v_ref.1) | copy-start | bytes 196612
  2.7 0.7 %copy-start.3 = (s32[16]{0:T(128)S(1)}, s32[16]{0:T(128)}, u32[]{:S(2)}) copy-start(s32[16]{0:T(128)} %lens_ref.1) | copy-start | bytes 196

commit v2 on v1

--- a/solution.py
+++ b/solution.py
@@ -198,16 +198,23 @@
         arrived(vbuf, row, 1, 0, mate_sem, theirs)
         attend(kbuf[row, :shard, :], vbuf[row, :shard, :], row * n_col * shard, False)
 
+    def relay(j):
+        source = source_of(j)
+
+        @pl.when((j < steps) & needs(row, source))
+        def _():
+            for which, buf in enumerate((kbuf, vbuf)):
+                arrived(buf, source, which, j, in_sem, mine)
+                forward(buf.at[source, mine, :], buf, source, which, j, j % 2 == 0)
+
     @pl.loop(1, steps)
     def _(j):
+        relay(2 * j - 1)
+        relay(2 * j)
         source = source_of(j)
 
         @pl.when(needs(row, source))
         def _():
-            straight = j % 2 == 0
-            for which, buf in enumerate((kbuf, vbuf)):
-                arrived(buf, source, which, j, in_sem, mine)
-                forward(buf.at[source, mine, :], buf, source, which, j, straight)
             arrived(kbuf, source, 0, j, mate_sem, theirs)
             arrived(vbuf, source, 1, j, mate_sem, theirs)
             attend(kbuf[source], vbuf[source], source * n_col * shard, False)
@@ -266,7 +273,7 @@
             sems,
         ],
         compiler_params=pltpu.CompilerParams(
-            collective_id=0, has_side_effects=True, vmem_limit_bytes=24 << 20
+            collective_id=0, has_side_effects=True, vmem_limit_bytes=60 << 20
         ),
         name="attend",
     )(doc_lengths, queries, keys, values)

time: 36.8 us -> 30 us (0.82)
  the two profiles are of different devices: /device:TPU:25 before, /device:TPU:24 now
where the time goes in v2:
time: 30 us; the launch traced here: 29.8 us
  Pallas kernels  28 us (93%)
  local copies, waits for them, and re-layouts  1.87 us (6%)
    pallas_call x1, Pallas kernels, shards(): pl.pallas_call(functools.partial(kernel, n_row, n_col, lanes, reach), out...  28 us
    unnamed x1, local copies, waits for them, and re-layouts  1.87 us

profile of v2, /device:TPU:24, one launch (start us, length us, event | category | flops | bytes accessed | tf_op | source)
XLA Modules:
  0.0 29.8 jit_solution(16872785388017275030)
XLA Ops:
  0.0 28.0 %attend.1 = bf16[256,1024]{1,0:T(8,128)(2,1)} custom-call(s32[16]{0:T(128)} %lens_ref.1, bf16[256,1024]{1,0:T(8,128)(2,1)} %q_ref.1, bf16[256,128]{1,0:T(8,128)(2,1)} %k_ref.1, bf16[256,128]{1,0:T(8,128)(2,1)} %v_ref.1), custom_call_target="tpu_custom_call" | custom-call | tf_op jit(solution)/shard_map/attend/pallas_call | solution.py:255
  28.0 1.9 %copy.6 = bf16[256,1024]{1,0:T(8,128)(2,1)} copy(bf16[256,1024]{1,0:T(8,128)(2,1)} %attend.1) | data formatting | bytes 1048576

commit v3 on v2

--- a/solution.py
+++ b/solution.py
@@ -10,6 +10,7 @@
 HEAD_DIM = 128
 RATE = HEAD_DIM ** (-0.5) * 1.4426950408889634
 MASKED = -1e30
+AHEAD_SLOTS = 8
 
 
 def kernel(
@@ -165,19 +166,19 @@
             )
             if fresh:
                 scores = scores + bias
-            s_ref[head % 2, :count, :] = scores
+            s_ref[head % AHEAD_SLOTS, :count, :] = scores
             top = jnp.max(scores, axis=0, keepdims=True)
             if fresh:
                 return top, top
             before = top_ref[head : head + 1, :]
             return before, jnp.maximum(before, top)
 
-        ahead = score(0)
+        tops = [score(head) for head in range(AHEAD_SLOTS - 1)]
         for head in range(heads):
-            before, top = ahead
-            if head + 1 < heads:
-                ahead = score(head + 1)
-            weights = jnp.exp2((s_ref[head % 2, :count, :] - top) * RATE)
+            before, top = tops[head]
+            if head + AHEAD_SLOTS - 1 < heads:
+                tops.append(score(head + AHEAD_SLOTS - 1))
+            weights = jnp.exp2((s_ref[head % AHEAD_SLOTS, :count, :] - top) * RATE)
             total = jnp.sum(weights, axis=0, keepdims=True)
             summed = jnp.dot(
                 vflip, weights.astype(jnp.bfloat16), preferred_element_type=jnp.float32
@@ -192,25 +193,26 @@
 
     attend(kbuf[row, mine, :], vbuf[row, mine, :], first, True)
 
+    def relay(j):
+        source = source_of(j)
+
+        @pl.when((j < steps) & needs(row, source))
+        def _():
+            for which, buf in enumerate((kbuf, vbuf)):
+                arrived(buf, source, which, j, in_sem, mine)
+                forward(buf.at[source, mine, :], buf, source, which, j, j % 2 == 0)
+
+    relay(1)
+    relay(2)
+
     @pl.when(col > 0)
     def _():
         arrived(kbuf, row, 0, 0, mate_sem, theirs)
         arrived(vbuf, row, 1, 0, mate_sem, theirs)
         attend(kbuf[row, :shard, :], vbuf[row, :shard, :], row * n_col * shard, False)
 
-    def relay(j):
-        source = source_of(j)
-
-        @pl.when((j < steps) & needs(row, source))
-        def _():
-            for which, buf in enumerate((kbuf, vbuf)):
-                arrived(buf, source, which, j, in_sem, mine)
-                forward(buf.at[source, mine, :], buf, source, which, j, j % 2 == 0)
-
     @pl.loop(1, steps)
     def _(j):
-        relay(2 * j - 1)
-        relay(2 * j)
         source = source_of(j)
 
         @pl.when(needs(row, source))
@@ -218,6 +220,9 @@
             arrived(kbuf, source, 0, j, mate_sem, theirs)
             arrived(vbuf, source, 1, j, mate_sem, theirs)
             attend(kbuf[source], vbuf[source], source * n_col * shard, False)
+
+        relay(2 * j + 1)
+        relay(2 * j + 2)
 
     for head in range(heads):
         inverse = 1.0 / total_ref[head : head + 1, :]
@@ -264,7 +269,7 @@
             pltpu.VMEM((heads, shard), jnp.float32),
             pltpu.VMEM((heads, HEAD_DIM, shard), jnp.float32),
             pltpu.VMEM((heads, shard, 2 * HEAD_DIM), queries.dtype),
-            pltpu.VMEM((2, tile, shard), jnp.float32),
+            pltpu.VMEM((AHEAD_SLOTS, tile, shard), jnp.float32),
             pltpu.SemaphoreType.DMA((2 + heads,)),
             sems,
             sems,

time: 30 us -> 29.5 us (0.983)
  Pallas kernels: 28 us -> 27.4 us
    pallas_call x1, Pallas kernels: 28 us -> 27.4 us  [shards(): pl.pallas_call(functools.partial(kernel, n_row, n_col, lanes, reach), out...]
where the time goes in v3:
time: 29.5 us; the launch traced here: 29.3 us
  Pallas kernels  27.4 us (93%)
  local copies, waits for them, and re-layouts  1.87 us (6%)
    pallas_call x1, Pallas kernels, shards(): pl.pallas_call(functools.partial(kernel, n_row, n_col, lanes, reach), out...  27.4 us
    unnamed x1, local copies, waits for them, and re-layouts  1.87 us

profile of v3, /device:TPU:24, one launch (start us, length us, event | category | flops | bytes accessed | tf_op | source)
XLA Modules:
  0.0 29.3 jit_solution(18210831601139851591)
XLA Ops:
  0.0 27.4 %attend.1 = bf16[256,1024]{1,0:T(8,128)(2,1)} custom-call(s32[16]{0:T(128)} %lens_ref.1, bf16[256,1024]{1,0:T(8,128)(2,1)} %q_ref.1, bf16[256,128]{1,0:T(8,128)(2,1)} %k_ref.1, bf16[256,128]{1,0:T(8,128)(2,1)} %v_ref.1), custom_call_target="tpu_custom_call" | custom-call | tf_op jit(solution)/shard_map/attend/pallas_call | solution.py:260
  27.4 1.9 %copy.6 = bf16[256,1024]{1,0:T(8,128)(2,1)} copy(bf16[256,1024]{1,0:T(8,128)(2,1)} %attend.1) | data formatting | bytes 1048576

commit v4 on v3

--- a/solution.py
+++ b/solution.py
@@ -193,17 +193,17 @@
 
     attend(kbuf[row, mine, :], vbuf[row, mine, :], first, True)
 
-    def relay(j):
+    def relay(j, least):
         source = source_of(j)
 
-        @pl.when((j < steps) & needs(row, source))
+        @pl.when((j >= least) & (j < steps) & needs(row, source))
         def _():
             for which, buf in enumerate((kbuf, vbuf)):
                 arrived(buf, source, which, j, in_sem, mine)
                 forward(buf.at[source, mine, :], buf, source, which, j, j % 2 == 0)
 
-    relay(1)
-    relay(2)
+    relay(jnp.int32(1), 1)
+    relay(jnp.int32(2), 1)
 
     @pl.when(col > 0)
     def _():
@@ -221,8 +221,9 @@
             arrived(vbuf, source, 1, j, mate_sem, theirs)
             attend(kbuf[source], vbuf[source], source * n_col * shard, False)
 
-        relay(2 * j + 1)
-        relay(2 * j + 2)
+        ahead = 2 * (j - jnp.where(lane == lanes - 1, 0, 1)) + 1
+        relay(ahead, 3)
+        relay(ahead + 1, 3)
 
     for head in range(heads):
         inverse = 1.0 / total_ref[head : head + 1, :]
@@ -278,10 +279,10 @@
             sems,
         ],
         compiler_params=pltpu.CompilerParams(
-            collective_id=0, has_side_effects=True, vmem_limit_bytes=60 << 20
+            collective_id=0, has_side_effects=True, vmem_limit_bytes=24 << 20
         ),
         name="attend",
-    )(doc_lengths, queries, keys, values)
+    )(*(pltpu.with_memory_space_constraint(x, pltpu.HBM) for x in (doc_lengths, queries, keys, values)))
 
 
 def solution(mesh):

time: 29.5 us -> 26.1 us (0.88)
  Pallas kernels: 27.4 us -> 25.1 us
  local copies, waits for them, and re-layouts: 1.87 us -> 0.8 us
    pallas_call x1, Pallas kernels: 27.4 us -> 25.1 us  [shards(): pl.pallas_call(functools.partial(kernel, n_row, n_col, lanes, reach), out...]
    unnamed x1, local copies, waits for them, and re-layouts: 1.87 us -> 0.8 us
where the time goes in v4:
time: 26.1 us; the launch traced here: 25.9 us
  Pallas kernels  25.1 us (96%)
  local copies, waits for them, and re-layouts  0.8 us (3%)
    pallas_call x1, Pallas kernels, shards(): pl.pallas_call(functools.partial(kernel, n_row, n_col, lanes, reach), out...  25.1 us
    unnamed x1, local copies, waits for them, and re-layouts  0.8 us

profile of v4, /device:TPU:24, one launch (start us, length us, event | category | flops | bytes accessed | tf_op | source)
XLA Modules:
  0.0 25.9 jit_solution(6494040871467254586)
XLA Ops:
  0.0 25.1 %attend.1 = bf16[256,1024]{1,0:T(8,128)(2,1)S(1)} custom-call(s32[16]{0:T(128)} %lens_ref.1, bf16[256,1024]{1,0:T(8,128)(2,1)} %q_ref.1, bf16[256,128]{1,0:T(8,128)(2,1)} %k_ref.1, bf16[256,128]{1,0:T(8,128)(2,1)} %v_ref.1), custom_call_target="tpu_custom_call" | custom-call | tf_op jit(solution)/shard_map/attend/pallas_call | solution.py:261
  25.1 0.8 %copy.6 = bf16[256,1024]{1,0:T(8,128)(2,1)} copy(bf16[256,1024]{1,0:T(8,128)(2,1)S(1)} %attend.1) | data formatting | bytes 1048576

commit v5 on v4

--- a/solution.py
+++ b/solution.py
@@ -222,8 +222,8 @@
             attend(kbuf[source], vbuf[source], source * n_col * shard, False)
 
         ahead = 2 * (j - jnp.where(lane == lanes - 1, 0, 1)) + 1
+        relay(ahead + 1, 3)
         relay(ahead, 3)
-        relay(ahead + 1, 3)
 
     for head in range(heads):
         inverse = 1.0 / total_ref[head : head + 1, :]

time: 26.1 us -> 24.6 us (0.943)
  Pallas kernels: 25.1 us -> 23.7 us
    pallas_call x1, Pallas kernels: 25.1 us -> 23.7 us  [shards(): pl.pallas_call(functools.partial(kernel, n_row, n_col, lanes, reach), out...]
where the time goes in v5:
time: 24.6 us; the launch traced here: 24.5 us
  Pallas kernels  23.7 us (96%)
  local copies, waits for them, and re-layouts  0.8 us (3%)
    pallas_call x1, Pallas kernels, shards(): pl.pallas_call(functools.partial(kernel, n_row, n_col, lanes, reach), out...  23.7 us
    unnamed x1, local copies, waits for them, and re-layouts  0.8 us

profile of v5, /device:TPU:24, one launch (start us, length us, event | category | flops | bytes accessed | tf_op | source)
XLA Modules:
  0.0 24.5 jit_solution(1523994795758665032)
XLA Ops:
  0.0 23.7 %attend.1 = bf16[256,1024]{1,0:T(8,128)(2,1)S(1)} custom-call(s32[16]{0:T(128)} %lens_ref.1, bf16[256,1024]{1,0:T(8,128)(2,1)} %q_ref.1, bf16[256,128]{1,0:T(8,128)(2,1)} %k_ref.1, bf16[256,128]{1,0:T(8,128)(2,1)} %v_ref.1), custom_call_target="tpu_custom_call" | custom-call | tf_op jit(solution)/shard_map/attend/pallas_call | solution.py:261
  23.7 0.8 %copy.6 = bf16[256,1024]{1,0:T(8,128)(2,1)} copy(bf16[256,1024]{1,0:T(8,128)(2,1)S(1)} %attend.1) | data formatting | bytes 1048576

commit v6 on v5

--- a/solution.py
+++ b/solution.py
@@ -202,8 +202,8 @@
                 arrived(buf, source, which, j, in_sem, mine)
                 forward(buf.at[source, mine, :], buf, source, which, j, j % 2 == 0)
 
+    relay(jnp.int32(2), 1)
     relay(jnp.int32(1), 1)
-    relay(jnp.int32(2), 1)
 
     @pl.when(col > 0)
     def _():

time: 24.6 us -> 24.1 us (0.980); the launches traced: 24.5 us -> 23.7 us
  Pallas kernels: 23.7 us -> 22.9 us
    pallas_call x1, Pallas kernels: 23.7 us -> 22.9 us  [shards(): pl.pallas_call(functools.partial(kernel, n_row, n_col, lanes, reach), out...]
where the time goes in v6:
time: 24.1 us; the launch traced here: 23.7 us
  Pallas kernels  22.9 us (95%)
  local copies, waits for them, and re-layouts  0.8 us (3%)
    pallas_call x1, Pallas kernels, shards(): pl.pallas_call(functools.partial(kernel, n_row, n_col, lanes, reach), out...  22.9 us
    unnamed x1, local copies, waits for them, and re-layouts  0.8 us

profile of v6, /device:TPU:24, one launch (start us, length us, event | category | flops | bytes accessed | tf_op | source)
XLA Modules:
  0.0 23.7 jit_solution(10878728420717347482)
XLA Ops:
  0.0 22.9 %attend.1 = bf16[256,1024]{1,0:T(8,128)(2,1)S(1)} custom-call(s32[16]{0:T(128)} %lens_ref.1, bf16[256,1024]{1,0:T(8,128)(2,1)} %q_ref.1, bf16[256,128]{1,0:T(8,128)(2,1)} %k_ref.1, bf16[256,128]{1,0:T(8,128)(2,1)} %v_ref.1), custom_call_target="tpu_custom_call" | custom-call | tf_op jit(solution)/shard_map/attend/pallas_call | solution.py:261
  22.9 0.8 %copy.6 = bf16[256,1024]{1,0:T(8,128)(2,1)} copy(bf16[256,1024]{1,0:T(8,128)(2,1)S(1)} %attend.1) | data formatting | bytes 1048576
